TPU v7x, 256 devices: a whole 4x4x8 slice. The times are simulated.
256 devices in a mesh: grp: 16 (over z_lo, y, core), dp: 16 (over x, z_hi).
Axes of the slice: x: 4, y: 4, z: 8 (z_hi: 4, z_lo: 2; z = z_hi * 2 + z_lo), core: 2. Of those that a mesh axis runs over, the one named last changes fastest.
Arguments:
- queries: bfloat16 [16, 16, 128, 2048], P('dp', 'grp'), may hold values from -18 to 18
- mem_keys: bfloat16 [16, 16, 256, 2048], P('dp', 'grp'), may hold values from -18 to 18
- mem_values: bfloat16 [16, 16, 256, 2048], P('dp', 'grp'), may hold values from -48 to 48
- lengths: int32 [16, 16], P('dp'), may hold values from 128 to 256, as said below
- mates: int32 [16, 16, 16], P('dp'), may hold values 0 or 1
- out_grad: bfloat16 [16, 16, 128, 2048], P('dp', 'grp'), may hold values from -6 to 6
- mlp_input: bfloat16 [16, 16, 128, 4096], P('dp', 'grp'), may hold values from -6 to 6
- gate_pre: bfloat16 [16, 16, 128, 5632], P('dp', 'grp'), may hold values from -6 to 6
- hidden_grad: bfloat16 [16, 16, 128, 5632], P('dp', 'grp'), may hold values from -0.03125 to 0.03125
Outputs:
- attn_out: bfloat16 [16, 16, 128, 2048], P('dp', 'grp')
- q_grad: bfloat16 [16, 16, 128, 2048], P('dp', 'grp')
- up_grad: float32 [4096, 5632], P(None, ('grp', 'dp'))
Inputs may be any that keep to these rules, and one draw needn't show every extreme that they name: `lengths`: each is a multiple of 128; in every group some document has 256. `mates`: A document reads its own previous context whatever its diagonal entry.
All inputs are finite; a program needn't handle non-finite values. No bound on the sum of `mates` on one device may be relied on, other than what follows from the above.
Results may differ from a plain program's by a relative error of at most 0.025.
Values may be sent and summed in bfloat16 or wider, within the bound.
No kernel may reach another device: no remote copies, remote signals or barrier semaphores. Data moves between devices by JAX's collectives and lax.ppermute only.
A program may use at most 128 MiB of HBM per device.

v0:
```python
import math
import jax
import jax.numpy as jnp
from jax import lax
from jax.sharding import Mesh
from jax.sharding import PartitionSpec as P

HEAD_DIM = 128
DP = ("dp_0", "dp_1")
GRP_DP = ("grp", "dp_0", "dp_1")


def summed_rows(x, axes, dim):
    if not axes:
        return x
    nearer = lax.psum_scatter(x, axes[0], scatter_dimension=dim, tiled=True)
    return summed_rows(nearer, axes[1:], dim)


def head_pass(query_head, key_head, value_head, grad_head, key_mask):
    inv_root = 1.0 / math.sqrt(query_head.shape[1])
    scores = jnp.dot(query_head, key_head.T, preferred_element_type=jnp.float32) * inv_root
    scores = jnp.where(key_mask, scores, -1e30)
    highest = jnp.max(scores, axis=1, keepdims=True)
    weights = jnp.exp(scores - highest)
    row_total = jnp.sum(weights, axis=1, keepdims=True)
    weights_bf = (weights / row_total).astype(jnp.bfloat16)
    result = jnp.dot(weights_bf, value_head, preferred_element_type=jnp.float32).astype(
        jnp.bfloat16
    )
    grad_weights = jnp.dot(grad_head, value_head.T, preferred_element_type=jnp.float32)
    row_dot = jnp.sum(
        grad_head.astype(jnp.float32) * result.astype(jnp.float32), axis=1, keepdims=True
    )
    grad_scores = (weights_bf.astype(jnp.float32) * (grad_weights - row_dot)).astype(jnp.bfloat16)
    grad_query = (
        jnp.dot(grad_scores, key_head, preferred_element_type=jnp.float32) * inv_root
    ).astype(jnp.bfloat16)
    return (result, grad_query)


def per_device(
    queries, mem_keys, mem_values, lengths, mates, out_grad, mlp_input, gate_pre, hidden_grad
):
    members = lax.axis_size("grp")
    rows_q = queries.shape[2]
    mem_rows = mem_keys.shape[2]
    heads_all = queries.shape[3] // HEAD_DIM
    local_heads = heads_all // members
    docs_block = max(1, min(members, 512 // rows_q))
    block_count = members // docs_block
    row_count = docs_block * rows_q
    allowed = (mates[0] > 0) | jnp.eye(members, dtype=bool)
    live_keys = jnp.arange(mem_rows, dtype=jnp.int32)[None, :] < lengths[0][:, None]

    def split_heads(block):
        return block[0, 0].reshape(block.shape[2], members, local_heads, HEAD_DIM)

    def per_head(pieces):
        query_head, key_head, value_head, grad_head = pieces

        def block_step(block_num):
            first_row = block_num * row_count
            query_rows = lax.dynamic_slice_in_dim(query_head, first_row, row_count, 0)
            grad_rows = lax.dynamic_slice_in_dim(grad_head, first_row, row_count, 0)
            allowed_rows = lax.dynamic_slice_in_dim(allowed, block_num * docs_block, docs_block, 0)
            key_mask = jnp.broadcast_to(
                allowed_rows[:, None, :, None] & live_keys[None, None, :, :],
                (docs_block, rows_q, members, mem_rows),
            )
            key_mask = key_mask.reshape(row_count, members * mem_rows)
            return head_pass(query_rows, key_head, value_head, grad_rows, key_mask)

        results, gradients = lax.map(block_step, jnp.arange(block_count))
        return (
            results.reshape(members * rows_q, HEAD_DIM),
            gradients.reshape(members * rows_q, HEAD_DIM),
        )

    exchanged = (
        lax.all_to_all(split_heads(queries), "grp", split_axis=1, concat_axis=0, tiled=True),
        lax.all_to_all(split_heads(mem_keys), "grp", split_axis=1, concat_axis=0, tiled=True),
        lax.all_to_all(split_heads(mem_values), "grp", split_axis=1, concat_axis=0, tiled=True),
        lax.all_to_all(split_heads(out_grad), "grp", split_axis=1, concat_axis=0, tiled=True),
    )
    query_all, key_all, value_all, grad_all = [
        jnp.moveaxis(member[:, 0], 1, 0) for member in exchanged
    ]
    results, gradients = lax.map(per_head, (query_all, key_all, value_all, grad_all))
    heads_out = jnp.moveaxis(results, 0, 1)[:, None]
    heads_grad = jnp.moveaxis(gradients, 0, 1)[:, None]
    back_out, back_grad = (
        lax.all_to_all(heads_out, "grp", split_axis=0, concat_axis=1, tiled=True),
        lax.all_to_all(heads_grad, "grp", split_axis=0, concat_axis=1, tiled=True),
    )
    attn_out = back_out.reshape(1, 1, rows_q, heads_all * HEAD_DIM)
    q_grad = back_grad.reshape(1, 1, rows_q, heads_all * HEAD_DIM)
    up_cot = (
        hidden_grad[0, 0].astype(jnp.float32) * jax.nn.silu(gate_pre[0, 0].astype(jnp.float32))
    ).astype(jnp.bfloat16)
    tokens = mlp_input[0, 0]
    contract = (((0,), (0,)), ((), ()))
    slices = lax.all_to_all(up_cot, "grp", split_axis=1, concat_axis=0, tiled=True)
    partial_value = lax.dot_general(
        lax.all_gather(tokens, "grp", axis=0, tiled=True),
        slices,
        contract,
        preferred_element_type=jnp.float32,
    )
    up_grad = summed_rows(partial_value.astype(jnp.bfloat16), DP, 1).astype(jnp.float32)
    return (attn_out, q_grad, up_grad)


def solution(mesh):
    finer = Mesh(mesh.devices.reshape(mesh.shape["grp"], 4, 4), ("grp", "dp_0", "dp_1"))
    return jax.shard_map(
        per_device,
        mesh=finer,
        in_specs=(
            P(DP, "grp", None, None),
            P(DP, "grp", None, None),
            P(DP, "grp", None, None),
            P(DP, None),
            P(DP, None, None),
            P(DP, "grp", None, None),
            P(DP, "grp", None, None),
            P(DP, "grp", None, None),
            P(DP, "grp", None, None),
        ),
        out_specs=(P(DP, "grp", None, None), P(DP, "grp", None, None), P(None, GRP_DP)),
        check_vma=False,
    )
```

profile of v0, /device:TPU:72, one launch (start us, length us, event | category | flops | bytes accessed | tf_op | source)
XLA Modules:
  0.0 324.0 jit_solution(11458148541503357170)
XLA Ops:
  9.9 6.3 %all-to-all-start.3 = ((bf16[128,16,1,128]{0,3,2,1:T(8,128)(2,1)}), bf16[128,16,1,128]{0,3,2,1:T(8,128)(2,1)S(1)}, u32[]{:S(2)}, u32[]{:S(2)}) async-start(bf16[128,16,1,128]{0,3,2,1:T(8,128)(2,1)} %bitcast.13), calls=%async_computation.3 | async-start | bytes 1048576 | tf_op jit(solution)/shard_map/all_to_all | solution.py:84
  18.6 4.9 %all-to-all-done.3 = bf16[128,16,1,128]{0,3,2,1:T(8,128)(2,1)S(1)} async-done(((bf16[128,16,1,128]{0,3,2,1:T(8,128)(2,1)}), bf16[128,16,1,128]{0,3,2,1:T(8,128)(2,1)S(1)}, u32[]{:S(2)}, u32[]{:S(2)}) %all-to-all-start.3) | async-done | bytes 524320 | tf_op jit(solution)/shard_map/all_to_all | solution.py:84
  23.4 7.1 %all-to-all-start = ((bf16[128,16,1,128]{3,0,2,1:T(8,128)(2,1)}), bf16[128,16,1,128]{3,0,2,1:T(8,128)(2,1)S(1)}, u32[]{:S(2)}, u32[]{:S(2)}) async-start(bf16[128,16,1,128]{3,0,2,1:T(8,128)(2,1)} %copy.51), calls=%async_computation | async-start | bytes 1048576 | tf_op jit(solution)/shard_map/all_to_all | solution.py:81
  32.4 9.4 %all-to-all-done = bf16[128,16,1,128]{3,0,2,1:T(8,128)(2,1)S(1)} async-done(((bf16[128,16,1,128]{3,0,2,1:T(8,128)(2,1)}), bf16[128,16,1,128]{3,0,2,1:T(8,128)(2,1)S(1)}, u32[]{:S(2)}, u32[]{:S(2)}) %all-to-all-start) | async-done | bytes 524320 | tf_op jit(solution)/shard_map/all_to_all | solution.py:81
  41.8 9.3 %all-to-all-start.2 = ((bf16[256,16,1,128]{3,0,2,1:T(8,128)(2,1)}), bf16[256,16,1,128]{3,0,2,1:T(8,128)(2,1)S(1)}, u32[]{:S(2)}, u32[]{:S(2)}) async-start(bf16[256,16,1,128]{3,0,2,1:T(8,128)(2,1)} %copy.55), calls=%async_computation.2 | async-start | bytes 2097152 | tf_op jit(solution)/shard_map/all_to_all | solution.py:83
  58.8 11.8 %all-to-all-done.2 = bf16[256,16,1,128]{3,0,2,1:T(8,128)(2,1)S(1)} async-done(((bf16[256,16,1,128]{3,0,2,1:T(8,128)(2,1)}), bf16[256,16,1,128]{3,0,2,1:T(8,128)(2,1)S(1)}, u32[]{:S(2)}, u32[]{:S(2)}) %all-to-all-start.2) | async-done | bytes 1048608 | tf_op jit(solution)/shard_map/all_to_all | solution.py:83
  70.6 12.9 %all-to-all-start.6 = ((bf16[128,16,352]{0,2,1:T(8,128)(2,1)}), bf16[128,16,352]{0,2,1:T(8,128)(2,1)}, u32[]{:S(2)}, u32[]{:S(2)}) async-start(bf16[128,16,352]{0,2,1:T(8,128)(2,1)} %fusion.23), calls=%async_computation.6 | async-start | bytes 2883584 | tf_op jit(solution)/shard_map/all_to_all | solution.py:103
  86.3 23.1 %all-to-all-done.6 = bf16[128,16,352]{0,2,1:T(8,128)(2,1)} async-done(((bf16[128,16,352]{0,2,1:T(8,128)(2,1)}), bf16[128,16,352]{0,2,1:T(8,128)(2,1)}, u32[]{:S(2)}, u32[]{:S(2)}) %all-to-all-start.6) | async-done | bytes 1441824 | tf_op jit(solution)/shard_map/all_to_all | solution.py:103
  109.4 14.3 %all-to-all-start.1 = ((bf16[256,16,1,128]{3,0,2,1:T(8,128)(2,1)}), bf16[256,16,1,128]{3,0,2,1:T(8,128)(2,1)S(1)}, u32[]{:S(2)}, u32[]{:S(2)}) async-start(bf16[256,16,1,128]{3,0,2,1:T(8,128)(2,1)} %copy.53), calls=%async_computation.1 | async-start | bytes 2097152 | tf_op jit(solution)/shard_map/all_to_all | solution.py:82
  124.9 24.6 %all-gather.3.cloned.1.call-done = bf16[1,1,2048,4096]{3,2,1,0:T(8,128)(2,1)} async-done(((bf16[1,1,128,4096]{3,2,1,0:T(8,128)(2,1)}), bf16[1,1,2048,4096]{3,2,1,0:T(8,128)(2,1)}) %all-gather.3.cloned.1.call-update) | async-done | bytes 16777232 | tf_op jit(solution)/shard_map/all_gather | solution.py:105
  149.5 13.4 %fusion.16 = bf16[4096,352]{0,1:T(8,128)(2,1)} fusion(bf16[1,1,2048,4096]{3,2,1,0:T(8,128)(2,1)} %all-gather.3.cloned.1.call-done, bf16[128,16,352]{0,2,1:T(8,128)(2,1)} %all-to-all-done.6), kind=kOutput, calls=%fused_computation.23 | convolution fusion | flops 5907021824 | bytes 21102592 | tf_op jit(solution)/shard_map/dot_general | solution.py:104
  163.0 92.8 %while.22 = (s32[]{:T(128)}, bf16[4,512,128]{2,1,0:T(8,128)(2,1)}, bf16[4,512,128]{2,1,0:T(8,128)(2,1)}, s32[4]{0:T(128)S(1)}, pred[16,16]{1,0:T(8,128)(4,1)S(1)...) while((s32[]{:T(128)}, bf16[4,512,128]{2,1,0:T(8,128)(2,1)}, ...), condition=%wide.region_4.5_spmd.clone, body=%wide.region_0.4_spmd.clone.sunk | while | flops 2173127168 | bytes 64675448 | solution.py:74
  176.5 3.7 %multiply_reduce_fusion.2 = (f32[512]{0:T(512)S(1)}, bf16[512,128]{0,1:T(8,128)(2,1)S(1)}) fusion(bf16[512,128]{0,1:T(8,128)(2,1)S(1)} %copy.86, bf16[512,4096]{1,0:T(8,128)(2,1)} %divide_convert_fusion.2, bf16[4096,128]{1,0:T(8,128)(2,1)S(1)} %get-tuple-element.299), kind=kOutput, calls=%fused_computation.12.clone.1 | convolution fusion | flops 537198080 | bytes 5507072 | tf_op jit(solution)/shard_map/while/body/eval_jaxpr/while/body/eval_jaxpr/dot_general | solution.py:28
  180.2 5.4 %fusion.52 = bf16[4,512,128]{2,1,0:T(8,128)(2,1)} fusion(bf16[4,512,128]{2,1,0:T(8,128)(2,1)} %get-tuple-element.278, s32[]{:T(128)} %get-tuple-element.276, bf16[4096,128]{1,0:T(8,128)(2,1)S(1)} %copy-done.2, bf16[512,4096]{1,0:T(8,128)(2,1)} %divide_convert_fusion.2, bf16[512,128]{1,0:T(8,128)(2,1)S(1)} %constant_dynamic-slice_fusion.4, ...), kind=kOutput, calls=%fused_computation.11.clone.1 | convolution fusion | flops 1082261504 | bytes 6556160 | tf_op jit(solution)/shard_map/while/body/eval_jaxpr/while/body/eval_jaxpr/dot_general | solution.py:37
  199.6 3.7 %multiply_reduce_fusion.2 = (f32[512]{0:T(512)S(1)}, bf16[512,128]{0,1:T(8,128)(2,1)S(1)}) fusion(bf16[512,128]{0,1:T(8,128)(2,1)S(1)} %copy.86, bf16[512,4096]{1,0:T(8,128)(2,1)} %divide_convert_fusion.2, bf16[4096,128]{1,0:T(8,128)(2,1)S(1)} %get-tuple-element.299), kind=kOutput, calls=%fused_computation.12.clone.1 | convolution fusion | flops 537198080 | bytes 5507072 | tf_op jit(solution)/shard_map/while/body/eval_jaxpr/while/body/eval_jaxpr/dot_general | solution.py:28
  203.4 5.4 %fusion.52 = bf16[4,512,128]{2,1,0:T(8,128)(2,1)} fusion(bf16[4,512,128]{2,1,0:T(8,128)(2,1)} %get-tuple-element.278, s32[]{:T(128)} %get-tuple-element.276, bf16[4096,128]{1,0:T(8,128)(2,1)S(1)} %copy-done.2, bf16[512,4096]{1,0:T(8,128)(2,1)} %divide_convert_fusion.2, bf16[512,128]{1,0:T(8,128)(2,1)S(1)} %constant_dynamic-slice_fusion.4, ...), kind=kOutput, calls=%fused_computation.11.clone.1 | convolution fusion | flops 1082261504 | bytes 6556160 | tf_op jit(solution)/shard_map/while/body/eval_jaxpr/while/body/eval_jaxpr/dot_general | solution.py:37
  222.8 3.7 %multiply_reduce_fusion.2 = (f32[512]{0:T(512)S(1)}, bf16[512,128]{0,1:T(8,128)(2,1)S(1)}) fusion(bf16[512,128]{0,1:T(8,128)(2,1)S(1)} %copy.86, bf16[512,4096]{1,0:T(8,128)(2,1)} %divide_convert_fusion.2, bf16[4096,128]{1,0:T(8,128)(2,1)S(1)} %get-tuple-element.299), kind=kOutput, calls=%fused_computation.12.clone.1 | convolution fusion | flops 537198080 | bytes 5507072 | tf_op jit(solution)/shard_map/while/body/eval_jaxpr/while/body/eval_jaxpr/dot_general | solution.py:28
  226.5 5.4 %fusion.52 = bf16[4,512,128]{2,1,0:T(8,128)(2,1)} fusion(bf16[4,512,128]{2,1,0:T(8,128)(2,1)} %get-tuple-element.278, s32[]{:T(128)} %get-tuple-element.276, bf16[4096,128]{1,0:T(8,128)(2,1)S(1)} %copy-done.2, bf16[512,4096]{1,0:T(8,128)(2,1)} %divide_convert_fusion.2, bf16[512,128]{1,0:T(8,128)(2,1)S(1)} %constant_dynamic-slice_fusion.4, ...), kind=kOutput, calls=%fused_computation.11.clone.1 | convolution fusion | flops 1082261504 | bytes 6556160 | tf_op jit(solution)/shard_map/while/body/eval_jaxpr/while/body/eval_jaxpr/dot_general | solution.py:37
  249.6 5.4 %fusion.52 = bf16[4,512,128]{2,1,0:T(8,128)(2,1)} fusion(bf16[4,512,128]{2,1,0:T(8,128)(2,1)} %get-tuple-element.278, s32[]{:T(128)} %get-tuple-element.276, bf16[4096,128]{1,0:T(8,128)(2,1)S(1)} %copy-done.2, bf16[512,4096]{1,0:T(8,128)(2,1)} %divide_convert_fusion.2, bf16[512,128]{1,0:T(8,128)(2,1)S(1)} %constant_dynamic-slice_fusion.4, ...), kind=kOutput, calls=%fused_computation.11.clone.1 | convolution fusion | flops 1082261504 | bytes 6556160 | tf_op jit(solution)/shard_map/while/body/eval_jaxpr/while/body/eval_jaxpr/dot_general | solution.py:37
  259.3 6.4 %all-to-all-start.4 = ((bf16[16,2,8192]{2,1,0:T(2,128)(2,1)}), bf16[16,2,8192]{2,1,0:T(2,128)(2,1)S(1)}, u32[]{:S(2)}, u32[]{:S(2)}) async-start(bf16[16,2,8192]{2,1,0:T(2,128)(2,1)} %reshape.67), calls=%async_computation.4 | async-start | bytes 1048576 | tf_op jit(solution)/shard_map/all_to_all | solution.py:93
  268.7 4.2 %all-to-all-done.4 = bf16[16,2,8192]{2,1,0:T(2,128)(2,1)S(1)} async-done(((bf16[16,2,8192]{2,1,0:T(2,128)(2,1)}), bf16[16,2,8192]{2,1,0:T(2,128)(2,1)S(1)}, u32[]{:S(2)}, u32[]{:S(2)}) %all-to-all-start.4) | async-done | bytes 524320 | tf_op jit(solution)/shard_map/all_to_all | solution.py:93
  272.9 7.1 %all-to-all-start.5 = ((bf16[16,2,8192]{2,1,0:T(2,128)(2,1)}), bf16[16,2,8192]{2,1,0:T(2,128)(2,1)S(1)}, u32[]{:S(2)}, u32[]{:S(2)}) async-start(bf16[16,2,8192]{2,1,0:T(2,128)(2,1)} %reshape.69), calls=%async_computation.5 | async-start | bytes 1048576 | tf_op jit(solution)/shard_map/all_to_all | solution.py:94
  280.0 25.5 %fusion.2 = bf16[4096,24]{0,1:T(8,128)(2,1)S(1)} fusion(bf16[4096,88]{0,1:T(8,128)(2,1)} %reduce-scatter.4.cloned.1.call-done), kind=kCustom, calls=%all-reduce-scatter | all-reduce-scatter fusion | flops 393217 | bytes 918528
  305.6 5.3 %collective-permute-start = (bf16[4096,6]{0,1:T(8,128)(2,1)S(1)}, bf16[4096,6]{0,1:T(8,128)(2,1)S(1)}, u32[]{:S(2)}, u32[]{:S(2)}) collective-permute-start(bf16[4096,6]{0,1:T(8,128)(2,1)S(1)} %slice), channel_id=1, source_target_pairs={{0,1},{1,2},{2,3},{4,5},{5,6},{6,7},{8,9},{9,10},{10,11},{12,13},{... | collective-permute-start | bytes 147464
  (133 shorter events, 85.2 us)
Async XLA Ops:
  7.2 23.4 %copy-start = (bf16[1,1,256,2048]{3,2,1,0:T(8,128)(2,1)S(1)}, bf16[1,1,256,2048]{3,2,1,0:T(8,128)(2,1)}, u32[]{:S(2)}) copy-start(bf16[1,1,256,2048]{3,2,1,0:T(8,128)(2,1)} %param.13) | copy-start | bytes 3145732
  7.2 142.3 %all-gather.3.cloned.1.call-start = ((), (), s32[]{:S(2)}) async-start(), calls=%async_computation.9 | async-start | bytes 17825792 | tf_op jit(solution)/shard_map/all_gather | solution.py:105
  9.9 13.5 %all-to-all-start.3 = ((bf16[128,16,1,128]{0,3,2,1:T(8,128)(2,1)}), bf16[128,16,1,128]{0,3,2,1:T(8,128)(2,1)S(1)}, u32[]{:S(2)}, u32[]{:S(2)}) async-start(bf16[128,16,1,128]{0,3,2,1:T(8,128)(2,1)} %bitcast.13), calls=%async_computation.3 | async-start | bytes 1048576 | tf_op jit(solution)/shard_map/all_to_all | solution.py:84
  23.4 18.3 %all-to-all-start = ((bf16[128,16,1,128]{3,0,2,1:T(8,128)(2,1)}), bf16[128,16,1,128]{3,0,2,1:T(8,128)(2,1)S(1)}, u32[]{:S(2)}, u32[]{:S(2)}) async-start(bf16[128,16,1,128]{3,0,2,1:T(8,128)(2,1)} %copy.51), calls=%async_computation | async-start | bytes 1048576 | tf_op jit(solution)/shard_map/all_to_all | solution.py:81
  41.8 28.8 %all-to-all-start.2 = ((bf16[256,16,1,128]{3,0,2,1:T(8,128)(2,1)}), bf16[256,16,1,128]{3,0,2,1:T(8,128)(2,1)S(1)}, u32[]{:S(2)}, u32[]{:S(2)}) async-start(bf16[256,16,1,128]{3,0,2,1:T(8,128)(2,1)} %copy.55), calls=%async_computation.2 | async-start | bytes 2097152 | tf_op jit(solution)/shard_map/all_to_all | solution.py:83
  58.8 65.0 %copy-start.6 = (s32[1,16,16]{2,1,0:T(8,128)S(1)}, s32[1,16,16]{2,1,0:T(8,128)}, u32[]{:S(2)}) copy-start(s32[1,16,16]{2,1,0:T(8,128)} %param.15) | copy-start | bytes 3076
  70.6 38.8 %all-to-all-start.6 = ((bf16[128,16,352]{0,2,1:T(8,128)(2,1)}), bf16[128,16,352]{0,2,1:T(8,128)(2,1)}, u32[]{:S(2)}, u32[]{:S(2)}) async-start(bf16[128,16,352]{0,2,1:T(8,128)(2,1)} %fusion.23), calls=%async_computation.6 | async-start | bytes 2883584 | tf_op jit(solution)/shard_map/all_to_all | solution.py:103
  109.4 53.5 %all-to-all-start.1 = ((bf16[256,16,1,128]{3,0,2,1:T(8,128)(2,1)}), bf16[256,16,1,128]{3,0,2,1:T(8,128)(2,1)S(1)}, u32[]{:S(2)}, u32[]{:S(2)}) async-start(bf16[256,16,1,128]{3,0,2,1:T(8,128)(2,1)} %copy.53), calls=%async_computation.1 | async-start | bytes 2097152 | tf_op jit(solution)/shard_map/all_to_all | solution.py:82
  123.7 156.3 %reduce-scatter.4.cloned.1.call-start = ((), (), s32[]{:S(2)}) async-start(), calls=%async_computation.8 | async-start | bytes 3604480 | tf_op jit(solution)/shard_map/reduce_scatter | solution.py:16
  124.9 38.1 %copy-start.5 = (s32[1,16]{1,0:T(1,128)S(1)}, s32[1,16]{1,0:T(1,128)}, u32[]{:S(2)}) copy-start(s32[1,16]{1,0:T(1,128)} %param.14) | copy-start | bytes 196
  163.2 2.1 copy-start.1
  163.2 2.1 copy-start.3
  175.3 4.9 %copy-start.2 = (bf16[4096,128]{1,0:T(8,128)(2,1)S(1)}, bf16[4096,128]{1,0:T(8,128)(2,1)}, u32[]{:S(2)}) copy-start(bf16[4096,128]{1,0:T(8,128)(2,1)} %copy-done.1) | copy-start | bytes 3145732 | tf_op jit(solution)/shard_map/while/body/eval_jaxpr/while
  180.2 6.2 %copy-start.4 = (bf16[2048,128]{1,0:T(8,128)(2,1)S(1)}, bf16[2048,128]{1,0:T(8,128)(2,1)}, u32[]{:S(2)}) copy-start(bf16[2048,128]{1,0:T(8,128)(2,1)} %copy-done.3) | copy-start | bytes 1572868 | tf_op jit(solution)/shard_map/while/body/eval_jaxpr/while
  198.5 4.9 %copy-start.2 = (bf16[4096,128]{1,0:T(8,128)(2,1)S(1)}, bf16[4096,128]{1,0:T(8,128)(2,1)}, u32[]{:S(2)}) copy-start(bf16[4096,128]{1,0:T(8,128)(2,1)} %copy-done.1) | copy-start | bytes 3145732 | tf_op jit(solution)/shard_map/while/body/eval_jaxpr/while
  203.4 6.2 %copy-start.4 = (bf16[2048,128]{1,0:T(8,128)(2,1)S(1)}, bf16[2048,128]{1,0:T(8,128)(2,1)}, u32[]{:S(2)}) copy-start(bf16[2048,128]{1,0:T(8,128)(2,1)} %copy-done.3) | copy-start | bytes 1572868 | tf_op jit(solution)/shard_map/while/body/eval_jaxpr/while
  221.7 4.8 %copy-start.2 = (bf16[4096,128]{1,0:T(8,128)(2,1)S(1)}, bf16[4096,128]{1,0:T(8,128)(2,1)}, u32[]{:S(2)}) copy-start(bf16[4096,128]{1,0:T(8,128)(2,1)} %copy-done.1) | copy-start | bytes 3145732 | tf_op jit(solution)/shard_map/while/body/eval_jaxpr/while
  226.5 6.2 %copy-start.4 = (bf16[2048,128]{1,0:T(8,128)(2,1)S(1)}, bf16[2048,128]{1,0:T(8,128)(2,1)}, u32[]{:S(2)}) copy-start(bf16[2048,128]{1,0:T(8,128)(2,1)} %copy-done.3) | copy-start | bytes 1572868 | tf_op jit(solution)/shard_map/while/body/eval_jaxpr/while
  244.8 4.8 %copy-start.2 = (bf16[4096,128]{1,0:T(8,128)(2,1)S(1)}, bf16[4096,128]{1,0:T(8,128)(2,1)}, u32[]{:S(2)}) copy-start(bf16[4096,128]{1,0:T(8,128)(2,1)} %copy-done.1) | copy-start | bytes 3145732 | tf_op jit(solution)/shard_map/while/body/eval_jaxpr/while
  249.6 6.2 %copy-start.4 = (bf16[2048,128]{1,0:T(8,128)(2,1)S(1)}, bf16[2048,128]{1,0:T(8,128)(2,1)}, u32[]{:S(2)}) copy-start(bf16[2048,128]{1,0:T(8,128)(2,1)} %copy-done.3) | copy-start | bytes 1572868 | tf_op jit(solution)/shard_map/while/body/eval_jaxpr/while
  255.8 55.1 %copy-start.7 = (u32[256]{0:T(256)S(1)}, u32[256]{0:T(256)}, u32[]{:S(2)}) copy-start(u32[256]{0:T(256)} %constant.63) | copy-start | bytes 3076
  259.3 13.6 %all-to-all-start.4 = ((bf16[16,2,8192]{2,1,0:T(2,128)(2,1)}), bf16[16,2,8192]{2,1,0:T(2,128)(2,1)S(1)}, u32[]{:S(2)}, u32[]{:S(2)}) async-start(bf16[16,2,8192]{2,1,0:T(2,128)(2,1)} %reshape.67), calls=%async_computation.4 | async-start | bytes 1048576 | tf_op jit(solution)/shard_map/all_to_all | solution.py:93
  272.9 41.2 %all-to-all-start.5 = ((bf16[16,2,8192]{2,1,0:T(2,128)(2,1)}), bf16[16,2,8192]{2,1,0:T(2,128)(2,1)S(1)}, u32[]{:S(2)}, u32[]{:S(2)}) async-start(bf16[16,2,8192]{2,1,0:T(2,128)(2,1)} %reshape.69), calls=%async_computation.5 | async-start | bytes 1048576 | tf_op jit(solution)/shard_map/all_to_all | solution.py:94
  305.6 10.4 %collective-permute-start = (bf16[4096,6]{0,1:T(8,128)(2,1)S(1)}, bf16[4096,6]{0,1:T(8,128)(2,1)S(1)}, u32[]{:S(2)}, u32[]{:S(2)}) collective-permute-start(bf16[4096,6]{0,1:T(8,128)(2,1)S(1)} %slice), channel_id=1, source_target_pairs={{0,1},{1,2},{2,3},{4,5},{5,6},{6,7},{8,9},{9,10},{10,11},{12,13},{... | collective-permute-start | bytes 147464
  (6 other events, 12.2 us)
Sparse Core Ops, SparseCore 0:
  9.8 139.5 all-gather.2
  163.1 40.1 reduce-scatter.3
where the time goes:
time: 325 us; the launch traced here: 324 us
  waiting for transfers between devices  78.7 us (24%)
  starting transfers between devices  68.8 us (21%)
  matrix products  62.7 us (19%)
  local copies, waits for them, and re-layouts  40.5 us (12%)
  other arithmetic  27.3 us (8%)
  blocking collectives  25.5 us (8%)
  between operations  14.9 us (5%)
  loops' own time  5.57 us (2%)
    unnamed x1, blocking collectives  25.5 us
    all_gather x1, waiting for transfers between devices, per_device(): lax.all_gather(tokens, 'grp', axis=0, tiled=True)  24.6 us
    all_to_all x1, waiting for transfers between devices, per_device(): lax.all_to_all(up_cot, 'grp', split_axis=1, concat_axis=0, tiled=True)  23.1 us
    dot_general x4, matrix products, head_pass(): jnp.dot(grad_scores, key_head, preferred_element_type=jnp.float32)  21.5 us
    unnamed x25, local copies, waits for them, and re-layouts  15.8 us
    dot_general x4, matrix products, head_pass(): jnp.dot(weights_bf, value_head, preferred_element_type=jnp.float32)  14.9 us
    all_to_all x1, starting transfers between devices, per_device(): lax.all_to_all(split_heads(mem_keys), 'grp', split_axis=1, concat_axis=0,...  14.3 us
    dot_general x1, matrix products, per_device(): lax.dot_general(lax.all_gather(tokens, 'grp', axis=0, tiled=True), slices...  13.4 us
  transfers between devices with their start and end apart: 10, of which 6 were waited for; matrix products, arithmetic and copies ran while one was open for 48% of the time, Pallas kernels for 0%

commit v1 on v0

--- a/solution.py
+++ b/solution.py
@@ -8,6 +8,11 @@
 HEAD_DIM = 128
 DP = ("dp_0", "dp_1")
 GRP_DP = ("grp", "dp_0", "dp_1")
+
+
+def swapped_in(x, axis, d):
+    sent = jnp.stack([x] * lax.axis_size(axis))
+    return jnp.concatenate(lax.all_to_all(sent, axis, 0, 0), axis=d)
 
 
 def summed_rows(x, axes, dim):
@@ -102,10 +107,7 @@
     contract = (((0,), (0,)), ((), ()))
     slices = lax.all_to_all(up_cot, "grp", split_axis=1, concat_axis=0, tiled=True)
     partial_value = lax.dot_general(
-        lax.all_gather(tokens, "grp", axis=0, tiled=True),
-        slices,
-        contract,
-        preferred_element_type=jnp.float32,
+        swapped_in(tokens, "grp", 0), slices, contract, preferred_element_type=jnp.float32
     )
     up_grad = summed_rows(partial_value.astype(jnp.bfloat16), DP, 1).astype(jnp.float32)
     return (attn_out, q_grad, up_grad)

time: 325 us -> 542 us (1.67)
  waiting for transfers between devices: 78.7 us -> 277 us
  blocking collectives: 25.5 us -> 46.3 us
  starting transfers between devices: 68.8 us -> 54.8 us
  local copies, waits for them, and re-layouts: 40.5 us -> 48.9 us
    all_to_all x1, waiting for transfers between devices: 23.1 us -> 255 us  [swapped_in(): return jnp.concatenate(lax.all_to_all(sent, axis, 0, 0), axis=d)]
    all_gather x1 -> x0, waiting for transfers between devices: 24.6 us -> none  [per_device(): lax.all_gather(tokens, 'grp', axis=0, tiled=True)]
    all_to_all x0 -> x1, blocking collectives: none -> 24.1 us  [per_device(): lax.all_to_all(up_cot, 'grp', split_axis=1, concat_axis=0, tiled=True)]
    all_to_all x1, starting transfers between devices: 14.3 us -> 7.17 us  [per_device(): lax.all_to_all(split_heads(mem_keys), 'grp', split_axis=1, concat_axis=0,...]
    all_to_all x1, waiting for transfers between devices: 11.8 us -> 4.89 us  [per_device(): lax.all_to_all(split_heads(mem_values), 'grp', split_axis=1, concat_axis=...]
    another operation x0 -> x1, local copies, waits for them, and re-layouts: none -> 6.85 us  [swapped_in(): sent = jnp.stack([x] * lax.axis_size(axis))]
    unnamed x25 -> x23, local copies, waits for them, and re-layouts: 15.8 us -> 12.3 us
  transfers between devices with their start and end apart: 10 -> 9, of which waited for: 6 -> 7; matrix products, arithmetic and copies ran while one was open for 48% -> 28% of each run, Pallas kernels for 0% -> 0%
where the time goes in v1:
time: 542 us; the launch traced here: 537 us
  waiting for transfers between devices  277 us (51%)
  matrix products  61.9 us (11%)
  starting transfers between devices  54.8 us (10%)
  local copies, waits for them, and re-layouts  48.9 us (9%)
  blocking collectives  46.3 us (9%)
  other arithmetic  27.3 us (5%)
  between operations  14.9 us (3%)
  loops' own time  5.9 us (1%)
    all_to_all x1, waiting for transfers between devices, swapped_in(): return jnp.concatenate(lax.all_to_all(sent, axis, 0, 0), axis=d)  255 us
    all_to_all x1, blocking collectives, per_device(): lax.all_to_all(up_cot, 'grp', split_axis=1, concat_axis=0, tiled=True)  24.1 us
    dot_general x4, matrix products, head_pass(): jnp.dot(grad_scores, key_head, preferred_element_type=jnp.float32)  22.7 us
    unnamed x1, blocking collectives  22.2 us
    dot_general x4, matrix products, head_pass(): jnp.dot(weights_bf, value_head, preferred_element_type=jnp.float32)  14.9 us
    convert_element_type x4, other arithmetic, head_pass(): weights_bf = (weights / row_total).astype(jnp.bfloat16)  13.2 us
    dot_general x4, matrix products, head_pass(): jnp.dot(query_head, key_head.T, preferred_element_type=jnp.float32)  13 us
    unnamed x23, local copies, waits for them, and re-layouts  12.3 us
  transfers between devices with their start and end apart: 9, of which 7 were waited for; matrix products, arithmetic and copies ran while one was open for 28% of the time, Pallas kernels for 0%

profile of v1, /device:TPU:72, one launch (start us, length us, event | category | flops | bytes accessed | tf_op | source)
XLA Modules:
  0.0 537.1 jit_solution(18165489732335269852)
XLA Ops:
  9.2 6.3 %all-to-all-start.3 = ((bf16[128,16,1,128]{0,3,2,1:T(8,128)(2,1)}), bf16[128,16,1,128]{0,3,2,1:T(8,128)(2,1)S(1)}, u32[]{:S(2)}, u32[]{:S(2)}) async-start(bf16[128,16,1,128]{0,3,2,1:T(8,128)(2,1)} %bitcast.13), calls=%async_computation.3 | async-start | bytes 1048576 | tf_op jit(solution)/shard_map/all_to_all | solution.py:89
  17.8 4.9 all-to-all-done.3
  22.7 7.1 %all-to-all-start = ((bf16[128,16,1,128]{3,0,2,1:T(8,128)(2,1)}), bf16[128,16,1,128]{3,0,2,1:T(8,128)(2,1)S(1)}, u32[]{:S(2)}, u32[]{:S(2)}) async-start(bf16[128,16,1,128]{3,0,2,1:T(8,128)(2,1)} %copy.50), calls=%async_computation | async-start | bytes 1048576 | tf_op jit(solution)/shard_map/all_to_all | solution.py:86
  32.6 4.5 all-to-all-done
  37.1 7.1 %all-to-all-start.2 = ((bf16[256,16,1,128]{3,0,2,1:T(8,128)(2,1)}), bf16[256,16,1,128]{3,0,2,1:T(8,128)(2,1)S(1)}, u32[]{:S(2)}, u32[]{:S(2)}) async-start(bf16[256,16,1,128]{3,0,2,1:T(8,128)(2,1)} %copy.54), calls=%async_computation.2 | async-start | bytes 2097152 | tf_op jit(solution)/shard_map/all_to_all | solution.py:88
  52.7 4.9 all-to-all-done.2
  57.6 24.1 %all_to_all.108 = bf16[128,16,352]{0,2,1:T(8,128)(2,1)} all-to-all(bf16[128,16,352]{0,2,1:T(8,128)(2,1)S(1)} %multiply_convert_fusion.1), channel_id=1, replica_groups=mesh['grp'=16,'dp_0'=4,'dp_1'=4] {'grp'}, dimensions={1} | all-to-all | bytes 2883584 | tf_op jit(solution)/shard_map/all_to_all | solution.py:108
  81.7 6.9 %stack.3 = bf16[16,128,4096]{2,1,0:T(8,128)(2,1)} broadcast(bf16[128,4096]{1,0:T(8,128)(2,1)} %bitcast.109), dimensions={1,2} | broadcast | bytes 17825792 | tf_op jit(solution)/shard_map/stack | solution.py:14
  88.5 8.1 %all-to-all-start.7 = ((bf16[16,128,4096]{2,1,0:T(8,128)(2,1)}), bf16[16,128,4096]{2,1,0:T(8,128)(2,1)}, u32[]{:S(2)}, u32[]{:S(2)}) async-start(bf16[16,128,4096]{2,1,0:T(8,128)(2,1)} %stack.3), calls=%async_computation.7 | async-start | bytes 33554432 | tf_op jit(solution)/shard_map/all_to_all | solution.py:15
  100.5 255.4 %all-to-all-done.7 = bf16[16,128,4096]{2,1,0:T(8,128)(2,1)} async-done(((bf16[16,128,4096]{2,1,0:T(8,128)(2,1)}), bf16[16,128,4096]{2,1,0:T(8,128)(2,1)}, u32[]{:S(2)}, u32[]{:S(2)}) %all-to-all-start.7) | async-done | bytes 16777248 | tf_op jit(solution)/shard_map/all_to_all | solution.py:15
  356.0 7.2 %all-to-all-start.1 = ((bf16[256,16,1,128]{3,0,2,1:T(8,128)(2,1)}), bf16[256,16,1,128]{3,0,2,1:T(8,128)(2,1)}, u32[]{:S(2)}, u32[]{:S(2)}) async-start(bf16[256,16,1,128]{3,0,2,1:T(8,128)(2,1)} %copy.52), calls=%async_computation.1 | async-start | bytes 2097152 | tf_op jit(solution)/shard_map/all_to_all | solution.py:87
  363.2 11.3 %fusion.12 = bf16[4096,352]{0,1:T(8,128)(2,1)} fusion(bf16[16,128,4096]{2,1,0:T(8,128)(2,1)} %all-to-all-done.7, bf16[128,16,352]{0,2,1:T(8,128)(2,1)} %all_to_all.108), kind=kOutput, calls=%fused_computation.22 | convolution fusion | flops 5907021824 | bytes 21102592 | tf_op jit(solution)/shard_map/dot_general | solution.py:109
  376.6 94.4 %while.22 = (s32[]{:T(128)}, bf16[4,512,128]{2,1,0:T(8,128)(2,1)}, bf16[4,512,128]{2,1,0:T(8,128)(2,1)}, s32[4]{0:T(128)S(1)}, pred[16,16]{1,0:T(8,128)(4,1)S(1)...) while((s32[]{:T(128)}, bf16[4,512,128]{2,1,0:T(8,128)(2,1)}, ...), condition=%wide.region_4.5_spmd.clone, body=%wide.region_0.4_spmd.clone.sunk | while | flops 2173127168 | bytes 56286784 | solution.py:79
  393.8 5.7 %fusion.40 = bf16[4,512,128]{2,1,0:T(8,128)(2,1)} fusion(bf16[4,512,128]{2,1,0:T(8,128)(2,1)} %get-tuple-element.278, s32[]{:T(128)} %get-tuple-element.276, bf16[4096,128]{1,0:T(8,128)(2,1)} %get-tuple-element.298, bf16[512,4096]{1,0:T(8,128)(2,1)} %divide_convert_fusion.2, bf16[512,128]{1,0:T(8,128)(2,1)S(1)} %constant_dynamic-slice_fusion.4, ...), kind=kOutput, calls=%fused_computation.11.clone.1 | convolution fusion | flops 1082261504 | bytes 6556160 | tf_op jit(solution)/shard_map/while/body/eval_jaxpr/while/body/eval_jaxpr/dot_general | solution.py:42
  413.7 3.8 multiply_reduce_fusion.2
  417.5 5.7 %fusion.40 = bf16[4,512,128]{2,1,0:T(8,128)(2,1)} fusion(bf16[4,512,128]{2,1,0:T(8,128)(2,1)} %get-tuple-element.278, s32[]{:T(128)} %get-tuple-element.276, bf16[4096,128]{1,0:T(8,128)(2,1)} %get-tuple-element.298, bf16[512,4096]{1,0:T(8,128)(2,1)} %divide_convert_fusion.2, bf16[512,128]{1,0:T(8,128)(2,1)S(1)} %constant_dynamic-slice_fusion.4, ...), kind=kOutput, calls=%fused_computation.11.clone.1 | convolution fusion | flops 1082261504 | bytes 6556160 | tf_op jit(solution)/shard_map/while/body/eval_jaxpr/while/body/eval_jaxpr/dot_general | solution.py:42
  437.3 3.7 multiply_reduce_fusion.2
  441.0 5.7 %fusion.40 = bf16[4,512,128]{2,1,0:T(8,128)(2,1)} fusion(bf16[4,512,128]{2,1,0:T(8,128)(2,1)} %get-tuple-element.278, s32[]{:T(128)} %get-tuple-element.276, bf16[4096,128]{1,0:T(8,128)(2,1)} %get-tuple-element.298, bf16[512,4096]{1,0:T(8,128)(2,1)} %divide_convert_fusion.2, bf16[512,128]{1,0:T(8,128)(2,1)S(1)} %constant_dynamic-slice_fusion.4, ...), kind=kOutput, calls=%fused_computation.11.clone.1 | convolution fusion | flops 1082261504 | bytes 6556160 | tf_op jit(solution)/shard_map/while/body/eval_jaxpr/while/body/eval_jaxpr/dot_general | solution.py:42
  464.6 5.7 %fusion.40 = bf16[4,512,128]{2,1,0:T(8,128)(2,1)} fusion(bf16[4,512,128]{2,1,0:T(8,128)(2,1)} %get-tuple-element.278, s32[]{:T(128)} %get-tuple-element.276, bf16[4096,128]{1,0:T(8,128)(2,1)} %get-tuple-element.298, bf16[512,4096]{1,0:T(8,128)(2,1)} %divide_convert_fusion.2, bf16[512,128]{1,0:T(8,128)(2,1)S(1)} %constant_dynamic-slice_fusion.4, ...), kind=kOutput, calls=%fused_computation.11.clone.1 | convolution fusion | flops 1082261504 | bytes 6556160 | tf_op jit(solution)/shard_map/while/body/eval_jaxpr/while/body/eval_jaxpr/dot_general | solution.py:42
  474.5 6.6 %all-to-all-start.4 = ((bf16[16,2,8192]{2,1,0:T(2,128)(2,1)}), bf16[16,2,8192]{2,1,0:T(2,128)(2,1)S(1)}, u32[]{:S(2)}, u32[]{:S(2)}) async-start(bf16[16,2,8192]{2,1,0:T(2,128)(2,1)} %reshape.70), calls=%async_computation.4 | async-start | bytes 1048576 | tf_op jit(solution)/shard_map/all_to_all | solution.py:98
  484.1 4.3 all-to-all-done.4
  488.5 7.1 %all-to-all-start.5 = ((bf16[16,2,8192]{2,1,0:T(2,128)(2,1)}), bf16[16,2,8192]{2,1,0:T(2,128)(2,1)S(1)}, u32[]{:S(2)}, u32[]{:S(2)}) async-start(bf16[16,2,8192]{2,1,0:T(2,128)(2,1)} %reshape.72), calls=%async_computation.5 | async-start | bytes 1048576 | tf_op jit(solution)/shard_map/all_to_all | solution.py:99
  495.5 22.2 %fusion.2 = bf16[4096,24]{0,1:T(8,128)(2,1)S(1)} fusion(bf16[4096,88]{0,1:T(8,128)(2,1)} %reduce-scatter.4.cloned.1.call-done), kind=kCustom, calls=%all-reduce-scatter | all-reduce-scatter fusion | flops 393217 | bytes 918528
  517.8 5.3 collective-permute-start
  (116 shorter events, 92.9 us)
Async XLA Ops:
  9.2 13.5 %all-to-all-start.3 = ((bf16[128,16,1,128]{0,3,2,1:T(8,128)(2,1)}), bf16[128,16,1,128]{0,3,2,1:T(8,128)(2,1)S(1)}, u32[]{:S(2)}, u32[]{:S(2)}) async-start(bf16[128,16,1,128]{0,3,2,1:T(8,128)(2,1)} %bitcast.13), calls=%async_computation.3 | async-start | bytes 1048576 | tf_op jit(solution)/shard_map/all_to_all | solution.py:89
  16.8 27.4 %copy-start = (bf16[1,1,128,5632]{3,2,1,0:T(8,128)(2,1)S(1)}, bf16[1,1,128,5632]{3,2,1,0:T(8,128)(2,1)}, u32[]{:S(2)}) copy-start(bf16[1,1,128,5632]{3,2,1,0:T(8,128)(2,1)} %param.19) | copy-start | bytes 4325380
  22.7 14.4 %all-to-all-start = ((bf16[128,16,1,128]{3,0,2,1:T(8,128)(2,1)}), bf16[128,16,1,128]{3,0,2,1:T(8,128)(2,1)S(1)}, u32[]{:S(2)}, u32[]{:S(2)}) async-start(bf16[128,16,1,128]{3,0,2,1:T(8,128)(2,1)} %copy.50), calls=%async_computation | async-start | bytes 1048576 | tf_op jit(solution)/shard_map/all_to_all | solution.py:86
  37.1 20.5 %all-to-all-start.2 = ((bf16[256,16,1,128]{3,0,2,1:T(8,128)(2,1)}), bf16[256,16,1,128]{3,0,2,1:T(8,128)(2,1)S(1)}, u32[]{:S(2)}, u32[]{:S(2)}) async-start(bf16[256,16,1,128]{3,0,2,1:T(8,128)(2,1)} %copy.54), calls=%async_computation.2 | async-start | bytes 2097152 | tf_op jit(solution)/shard_map/all_to_all | solution.py:88
  88.5 267.4 %all-to-all-start.7 = ((bf16[16,128,4096]{2,1,0:T(8,128)(2,1)}), bf16[16,128,4096]{2,1,0:T(8,128)(2,1)}, u32[]{:S(2)}, u32[]{:S(2)}) async-start(bf16[16,128,4096]{2,1,0:T(8,128)(2,1)} %stack.3), calls=%async_computation.7 | async-start | bytes 33554432 | tf_op jit(solution)/shard_map/all_to_all | solution.py:15
  96.6 2.9 copy-start.4
  356.0 20.7 %all-to-all-start.1 = ((bf16[256,16,1,128]{3,0,2,1:T(8,128)(2,1)}), bf16[256,16,1,128]{3,0,2,1:T(8,128)(2,1)}, u32[]{:S(2)}, u32[]{:S(2)}) async-start(bf16[256,16,1,128]{3,0,2,1:T(8,128)(2,1)} %copy.52), calls=%async_computation.1 | async-start | bytes 2097152 | tf_op jit(solution)/shard_map/all_to_all | solution.py:87
  363.1 13.5 %copy-start.3 = (s32[1,16]{1,0:T(1,128)S(1)}, s32[1,16]{1,0:T(1,128)}, u32[]{:S(2)}) copy-start(s32[1,16]{1,0:T(1,128)} %param.14) | copy-start | bytes 196
  363.1 132.4 %reduce-scatter.4.cloned.1.call-start = ((), (), s32[]{:S(2)}) async-start(), calls=%async_computation.9 | async-start | bytes 3604480 | tf_op jit(solution)/shard_map/reduce_scatter | solution.py:21
  376.6 2.2 copy-start.1
  393.8 6.5 %copy-start.2 = (bf16[2048,128]{1,0:T(8,128)(2,1)S(1)}, bf16[2048,128]{1,0:T(8,128)(2,1)}, u32[]{:S(2)}) copy-start(bf16[2048,128]{1,0:T(8,128)(2,1)} %copy-done.1) | copy-start | bytes 1572868 | tf_op jit(solution)/shard_map/while/body/eval_jaxpr/while
  400.3 2.2 copy-start.1
  417.5 6.5 %copy-start.2 = (bf16[2048,128]{1,0:T(8,128)(2,1)S(1)}, bf16[2048,128]{1,0:T(8,128)(2,1)}, u32[]{:S(2)}) copy-start(bf16[2048,128]{1,0:T(8,128)(2,1)} %copy-done.1) | copy-start | bytes 1572868 | tf_op jit(solution)/shard_map/while/body/eval_jaxpr/while
  423.9 2.2 copy-start.1
  441.0 6.5 %copy-start.2 = (bf16[2048,128]{1,0:T(8,128)(2,1)S(1)}, bf16[2048,128]{1,0:T(8,128)(2,1)}, u32[]{:S(2)}) copy-start(bf16[2048,128]{1,0:T(8,128)(2,1)} %copy-done.1) | copy-start | bytes 1572868 | tf_op jit(solution)/shard_map/while/body/eval_jaxpr/while
  447.5 2.2 copy-start.1
  464.6 6.5 %copy-start.2 = (bf16[2048,128]{1,0:T(8,128)(2,1)S(1)}, bf16[2048,128]{1,0:T(8,128)(2,1)}, u32[]{:S(2)}) copy-start(bf16[2048,128]{1,0:T(8,128)(2,1)} %copy-done.1) | copy-start | bytes 1572868 | tf_op jit(solution)/shard_map/while/body/eval_jaxpr/while
  471.0 52.0 %copy-start.5 = (u32[256]{0:T(256)S(1)}, u32[256]{0:T(256)}, u32[]{:S(2)}) copy-start(u32[256]{0:T(256)} %constant.63) | copy-start | bytes 3076
  474.5 13.9 %all-to-all-start.4 = ((bf16[16,2,8192]{2,1,0:T(2,128)(2,1)}), bf16[16,2,8192]{2,1,0:T(2,128)(2,1)S(1)}, u32[]{:S(2)}, u32[]{:S(2)}) async-start(bf16[16,2,8192]{2,1,0:T(2,128)(2,1)} %reshape.70), calls=%async_computation.4 | async-start | bytes 1048576 | tf_op jit(solution)/shard_map/all_to_all | solution.py:98
  488.5 37.8 %all-to-all-start.5 = ((bf16[16,2,8192]{2,1,0:T(2,128)(2,1)}), bf16[16,2,8192]{2,1,0:T(2,128)(2,1)S(1)}, u32[]{:S(2)}, u32[]{:S(2)}) async-start(bf16[16,2,8192]{2,1,0:T(2,128)(2,1)} %reshape.72), calls=%async_computation.5 | async-start | bytes 1048576 | tf_op jit(solution)/shard_map/all_to_all | solution.py:99
  517.8 11.3 %collective-permute-start = (bf16[4096,6]{0,1:T(8,128)(2,1)S(1)}, bf16[4096,6]{0,1:T(8,128)(2,1)S(1)}, u32[]{:S(2)}, u32[]{:S(2)}) collective-permute-start(bf16[4096,6]{0,1:T(8,128)(2,1)S(1)} %slice), channel_id=1, source_target_pairs={{0,1},{1,2},{2,3},{4,5},{5,6},{6,7},{8,9},{9,10},{10,11},{12,13},{... | collective-permute-start | bytes 147464
Sparse Core Ops, SparseCore 0:
  374.6 39.7 reduce-scatter.3
